TPU v7x, 32 devices: a whole 2x2x4 slice. The times are simulated.
32 devices in a mesh: groups: 2 (over y), seq: 4 (over z), dp: 4 (over x, core).
Axes of the slice: x: 2, y: 2, z: 4, core: 2. Of those that a mesh axis runs over, the one named last changes fastest.
Arguments:
- inputs: bfloat16 [8, 32768, 768], P(('groups', 'dp'), 'seq'), parts along dimension 0, may hold values from -33 to 33, as said below
- norm_gain: float32 [768], replicated, may hold values from 0.5 to 1.5
- inner_mix: bfloat16 [256, 256], replicated, may hold values from -0.375 to 0.375
- twiddle: float32 [128, 256], P('seq'), may hold values from 0.5 to 2
- outer_mix: bfloat16 [128, 128], replicated, may hold values from -0.5 to 0.5
- long_kernel: float32 [128, 256], P(None, 'seq'), may hold values from 0.5 to 2
- gate_weight: bfloat16 [768, 384], replicated, may hold values from -0.3125 to 0.3125
- out_weight: bfloat16 [768, 384], replicated, may hold values from -0.3125 to 0.3125
- cotangent: bfloat16 [8, 32768, 768], P(('groups', 'dp'), 'seq'), parts along dimension 0, may hold values from -6 to 6
Outputs:
- layer_out: bfloat16 [8, 32768, 768], P(('groups', 'dp'), 'seq'), parts along dimension 0
- input_grad: bfloat16 [8, 32768, 768], P(('groups', 'dp'), 'seq'), parts along dimension 0
- weight_grads: float32 [3072, 384], P(('groups', 'seq')), parts along dimension 0
There are 2 independent parts, one for each index of `groups`. A program takes and returns all parts, laid end to end along the dimension named above; an argument that names none is the same for every part. Nothing has to cross between parts.
Inputs may be any that keep to these rules, and one draw needn't show every extreme that they name: `inputs`: activations' entries.
All inputs are finite; a program needn't handle non-finite values.
Results may differ from a plain program's by a relative error of at most 0.0072.
Values may be sent and summed in bfloat16 or wider, within the bound.
A program may use at most 384 MiB of HBM per device.

v0:
```python
import math
import jax
import jax.numpy as jnp
from jax import lax
from jax.sharding import PartitionSpec as P

norm_eps = 1e-06


def normalize(values, norm_gain):
    mean_square = jnp.mean(values * values, axis=-1, keepdims=True)
    return values * lax.rsqrt(mean_square + norm_eps) * norm_gain


def block_apply(operand, weight):
    blocks = weight.shape[0] // weight.shape[1]
    grouped = operand.reshape(operand.shape[0], blocks, weight.shape[1])
    stacked = weight.reshape(blocks, weight.shape[1], weight.shape[1])
    result = jnp.einsum("rki,kij->rkj", grouped, stacked, preferred_element_type=jnp.float32)
    return result.reshape(operand.shape[0], -1)


def block_back(partner, weight):
    blocks = weight.shape[0] // weight.shape[1]
    grouped = partner.reshape(partner.shape[0], blocks, weight.shape[1])
    stacked = weight.reshape(blocks, weight.shape[1], weight.shape[1])
    result = jnp.einsum("rkj,kij->rki", grouped, stacked, preferred_element_type=jnp.float32)
    return result.reshape(partner.shape[0], -1)


def block_term(operand, partner, blocks, block_size):
    grouped = operand.reshape(operand.shape[0], blocks, block_size)
    other_rows = partner.reshape(partner.shape[0], blocks, block_size)
    result = jnp.einsum("rki,rkj->kij", grouped, other_rows, preferred_element_type=jnp.float32)
    return result.reshape(blocks * block_size, block_size)


def to_columns(row_layout):
    return lax.all_to_all(row_layout, "seq", split_axis=2, concat_axis=1, tiled=True)


def to_rows(col_layout):
    return lax.all_to_all(col_layout, "seq", split_axis=1, concat_axis=2, tiled=True)


def shards(
    inputs,
    norm_gain,
    inner_mix,
    twiddle,
    outer_mix,
    long_kernel,
    gate_weight,
    out_weight,
    cotangent,
):
    batch_local, rows_local, channels = inputs.shape
    inner_len = inner_mix.shape[0]
    local_outer = rows_local // inner_len
    flat_rows = batch_local * rows_local
    block_size = gate_weight.shape[1]
    blocks = gate_weight.shape[0] // block_size
    all_tokens = batch_local * lax.axis_size("dp") * rows_local * lax.axis_size("seq")
    grad_scale = 1.0 / math.sqrt(all_tokens)
    inputs_wide = inputs.reshape(flat_rows, channels).astype(jnp.float32)
    activation = normalize(inputs_wide, norm_gain).astype(jnp.bfloat16)
    grid_rows = activation.reshape(batch_local, local_outer, inner_len, channels)
    inner_out = jnp.einsum(
        "jq,bpqd->bpjd", inner_mix, grid_rows, preferred_element_type=jnp.float32
    )
    mixed_rows = (inner_out * twiddle[None, :, :, None]).astype(jnp.bfloat16)
    columns = to_columns(mixed_rows)
    outer_out = jnp.einsum("ip,bpjd->bijd", outer_mix, columns, preferred_element_type=jnp.float32)
    mixed_cols = (outer_out * long_kernel[None, :, :, None]).astype(jnp.bfloat16)
    seq_mix = to_rows(mixed_cols).reshape(flat_rows, channels)
    gate_pre = block_apply(activation, gate_weight)
    gate_sig = jax.nn.sigmoid(gate_pre)
    mix_wide = seq_mix.astype(jnp.float32)
    gated_rows = (mix_wide * gate_pre * gate_sig).astype(jnp.bfloat16)
    layer_out = (inputs_wide + block_apply(gated_rows, out_weight)).astype(jnp.bfloat16)
    cotan_rows = cotangent.reshape(flat_rows, channels)
    back_gated = block_back(cotan_rows, out_weight)
    mix_grad = (back_gated * gate_pre * gate_sig).astype(jnp.bfloat16)
    gate_grad = (back_gated * mix_wide * gate_sig * (1.0 + gate_pre * (1.0 - gate_sig))).astype(
        jnp.bfloat16
    )
    act_grad = block_back(gate_grad, gate_weight)
    weight_term = jnp.concatenate(
        [
            block_term(activation, gate_grad, blocks, block_size),
            block_term(gated_rows, cotan_rows, blocks, block_size),
        ],
        axis=0,
    )
    grad_cols = to_columns(mix_grad.reshape(batch_local, local_outer, inner_len, channels))
    scaled_back = (grad_cols.astype(jnp.float32) * long_kernel[None, :, :, None]).astype(
        jnp.bfloat16
    )
    back_outer = jnp.einsum(
        "ip,bijd->bpjd", outer_mix, scaled_back, preferred_element_type=jnp.float32
    ).astype(jnp.bfloat16)
    back_rows = to_rows(back_outer)
    twisted = (back_rows.astype(jnp.float32) * twiddle[None, :, :, None]).astype(jnp.bfloat16)
    inner_back = jnp.einsum("jq,bpjd->bpqd", inner_mix, twisted, preferred_element_type=jnp.float32)
    act_grad = act_grad + inner_back.reshape(flat_rows, channels)
    pullback = jax.vjp(lambda wide_rows: normalize(wide_rows, norm_gain), inputs_wide)[1]
    input_grad = (cotan_rows.astype(jnp.float32) + pullback(act_grad)[0]).astype(jnp.bfloat16)
    shard_term = lax.psum_scatter(weight_term, "seq", scatter_dimension=0, tiled=True)
    weight_grads = lax.psum(shard_term, "dp") * grad_scale
    return (layer_out.reshape(inputs.shape), input_grad.reshape(inputs.shape), weight_grads)


def solution(mesh):
    return jax.shard_map(
        shards,
        mesh=mesh,
        in_specs=(
            P(("groups", "dp"), "seq", None),
            P(),
            P(),
            P("seq", None),
            P(),
            P(None, "seq"),
            P(),
            P(),
            P(("groups", "dp"), "seq", None),
        ),
        out_specs=(
            P(("groups", "dp"), "seq", None),
            P(("groups", "dp"), "seq", None),
            P(("groups", "seq"), None),
        ),
        check_vma=False,
    )
```

profile of v0, /device:TPU:21, one launch (start us, length us, event | category | flops | bytes accessed | tf_op | source)
XLA Modules:
  0.0 1638.3 jit_solution(11999235351812838798)
XLA Ops:
  14.4 14.3 convert_element_type.135
  28.8 24.7 %copy.107 = f32[32,256,768]{1,2,0:T(8,128)} copy(f32[32,256,768]{2,1,0:T(8,128)} %bitcast.156) | data formatting | bytes 50331648 | tf_op jit(solution)/shard_map/convert_element_type | solution.py:65
  53.5 14.2 fusion.24
  67.6 16.6 %copy.108 = bf16[1,32,256,768]{3,1,0,2:T(8,128)(2,1)} copy(bf16[1,32,256,768]{2,3,1,0:T(8,128)(2,1)} %fusion.24) | data formatting | bytes 25165824 | tf_op jit(solution)/shard_map/convert_element_type | solution.py:71
  84.2 275.7 %all_to_all.42 = bf16[1,32,256,768]{3,1,0,2:T(8,128)(2,1)S(1)} all-to-all(bf16[1,32,256,768]{3,1,0,2:T(8,128)(2,1)} %copy.108), channel_id=1, replica_groups=mesh['groups'=2,'seq'=4,'dp'=4] {'seq'}, dimensions={2} | all-to-all | bytes 25165824 | tf_op jit(solution)/shard_map/all_to_all | solution.py:39
  359.9 16.4 %copy.109 = bf16[1,32,256,768]{3,2,1,0:T(8,128)(2,1)S(1)} copy(bf16[1,32,256,768]{3,1,0,2:T(8,128)(2,1)S(1)} %all_to_all.42) | data formatting | bytes 25165824 | tf_op jit(solution)/shard_map/all_to_all | solution.py:39
  381.6 24.2 %fusion.7 = bf16[1,128,64,768]{1,3,2,0:T(8,128)(2,1)} fusion(f32[128,64]{0,1:T(8,128)S(1)} %copy-done.12, bf16[128,64,768]{2,1,0:T(8,128)(2,1)} %bitcast.157, bf16[128,128]{1,0:T(8,128)(2,1)S(1)} %copy-done.16), kind=kOutput, calls=%fused_computation.14 | convolution fusion | flops 1623195648 | bytes 25231360 | tf_op jit(solution)/shard_map/ip,bpjd->bijd/dot_general | solution.py:73
  405.8 16.5 %copy.112 = bf16[1,128,64,768]{3,2,0,1:T(8,128)(2,1)} copy(bf16[1,128,64,768]{1,3,2,0:T(8,128)(2,1)} %fusion.7) | data formatting | bytes 25165824 | tf_op jit(solution)/shard_map/convert_element_type | solution.py:74
  430.4 17.6 %copy.142 = f32[1,8192,768]{1,2,0:T(8,128)} copy(bf16[1,8192,768]{2,1,0:T(8,128)(2,1)} %param.9) | data formatting | bytes 37748736 | tf_op jit(solution)/shard_map/convert_element_type | solution.py:65
  448.0 24.3 %reshape_reshape.4 = bf16[8192,2,384]{2,1,0:T(2,128)(2,1)} reshape(bf16[1,8192,768]{2,1,0:T(8,128)(2,1)} %param.17) | data formatting | bytes 25165824 | tf_op jit(solution)/shard_map/reshape;reshape | solution.py:25
  472.4 21.1 %fusion.41 = f32[2,8192,384]{2,1,0:T(8,128)} fusion(bf16[2,384,384]{2,1,0:T(8,128)(2,1)S(1)} %bitcast.163, f32[8192,2,384]{0,2,1:T(8,128)} %bitcast.152, f32[2,384]{1,0:T(2,128)S(1)} %mul.196, f32[8192]{0:T(1024)S(1)} %fusion.46), kind=kOutput, calls=%fused_computation.57 | convolution fusion | flops 4850712576 | bytes 50957312 | tf_op jit(solution)/shard_map/rki,kij->rkj/dot_general | solution.py:19
  493.5 206.3 %all-to-all-done.1 = bf16[1,128,64,768]{3,2,0,1:T(8,128)(2,1)} async-done(((bf16[1,128,64,768]{3,2,0,1:T(8,128)(2,1)}), bf16[1,128,64,768]{3,2,0,1:T(8,128)(2,1)}, u32[]{:S(2)}, u32[]{:S(2)}) %all-to-all-start.1) | async-done | bytes 12582944 | tf_op jit(solution)/shard_map/all_to_all | solution.py:43
  716.6 30.3 %reshape.272 = f32[8192,2,384]{2,1,0:T(2,128)} reshape(f32[1,32,4,64,768]{4,3,2,1,0:T(8,128)} %copy.114) | data formatting | bytes 50331648 | tf_op jit(solution)/shard_map/convert_element_type | solution.py:78
  746.9 39.9 %fusion.13 = (bf16[8192,2,384]{2,0,1:T(8,128)(2,1)}, bf16[8192,2,384]{2,0,1:T(8,128)(2,1)}, bf16[8192,2,384]{2,0,1:T(8,128)(2,1)}) fusion(f32[2,8192,384]{2,1,0:T(8,128)} %fusion.41, f32[8192,2,384]{2,1,0:T(2,128)} %reshape.272, bf16[2,384,384]{2,1,0:T(8,128)(2,1)S(1)} %bitcast.149, bf16[8192,2,384]{2,1,0:T(2,128)(2,1)} %reshape_reshape.4), kind=kOutput, calls=%fused_computation.23 | convolution fusion | flops 4932501504 | bytes 101253120 | tf_op jit(solution)/shard_map/rkj,kij->rki/dot_general | solution.py:27
  786.8 16.2 copy.123
  803.0 11.9 copy.144
  814.9 18.3 %copy.124 = bf16[1,32,256,768]{3,1,0,2:T(8,128)(2,1)} copy(bf16[1,32,256,768]{2,1,3,0:T(8,128)(2,1)} %bitcast.160) | data formatting | bytes 25165824 | tf_op jit(solution)/shard_map/convert_element_type | solution.py:83
  842.8 269.4 %all-to-all-done.2 = bf16[1,32,256,768]{3,1,0,2:T(8,128)(2,1)} async-done(((bf16[1,32,256,768]{3,1,0,2:T(8,128)(2,1)}), bf16[1,32,256,768]{3,1,0,2:T(8,128)(2,1)}, u32[]{:S(2)}, u32[]{:S(2)}) %all-to-all-start.2) | async-done | bytes 12582944 | tf_op jit(solution)/shard_map/all_to_all | solution.py:39
  1130.4 10.1 copy.126
  1146.6 22.8 %convert_bitcast_fusion.3 = bf16[1,128,64,768]{1,3,2,0:T(8,128)(2,1)} fusion(bf16[128,64,768]{2,1,0:T(8,128)(2,1)} %fusion.8, bf16[128,128]{1,0:T(8,128)(2,1)S(1)} %copy-done.17), kind=kOutput, calls=%fused_computation.49 | convolution fusion | flops 1616904192 | bytes 25198592 | tf_op jit(solution)/shard_map/ip,bijd->bpjd/dot_general | solution.py:99
  1169.4 16.7 %copy.129 = bf16[1,128,64,768]{3,2,0,1:T(8,128)(2,1)} copy(bf16[1,128,64,768]{1,3,2,0:T(8,128)(2,1)} %convert_bitcast_fusion.3) | data formatting | bytes 25165824 | tf_op jit(solution)/shard_map/convert_element_type | solution.py:101
  1195.5 13.9 fusion.32
  1209.5 15.7 fusion.40
  1226.8 14.6 fusion.48
  1241.5 204.8 %reduce-scatter.2.cloned.1.call-done = f32[384,384]{1,0:T(8,128)} async-done(((f32[1536,384]{1,0:T(8,128)}), f32[384,384]{1,0:T(8,128)}) %reduce-scatter.2.cloned.1.call-update) | async-done | bytes 589840 | tf_op jit(solution)/shard_map/reduce_scatter | solution.py:108
  1446.3 14.7 fusion.47
  1460.9 24.8 %copy.134 = f32[8192,768]{1,0:T(8,128)} copy(f32[8192,768]{0,1:T(8,128)} %bitcast.150) | data formatting | bytes 50331648 | tf_op jit(solution)/shard_map/reshape | solution.py:28
  1485.7 24.7 %copy.133 = f32[1,8192,768]{2,1,0:T(8,128)} copy(f32[1,8192,768]{1,2,0:T(8,128)} %bitcast.151) | data formatting | bytes 50331648 | tf_op jit(solution)/shard_map/reshape | solution.py:28
  1510.4 24.7 %copy.119 = f32[1,8192,768]{2,1,0:T(8,128)} copy(f32[1,8192,768]{1,2,0:T(8,128)} %bitcast.155) | data formatting | bytes 50331648 | tf_op jit(solution)/shard_map/reshape | solution.py:20
  1553.8 15.5 fusion.23
  1569.3 20.7 %fusion.4 = f32[8192]{0:T(1024)S(1)} fusion(f32[8192,768]{1,0:T(8,128)} %copy.134, f32[32,768,256]{1,2,0:T(8,128)} %fusion.23, bf16[1,8192,768]{2,1,0:T(8,128)(2,1)} %param.9, f32[768]{0:T(1024)S(1)} %copy-done.19), kind=kLoop, calls=%fused_computation.6 | loop fusion | flops 31449088 | bytes 62950400 | tf_op jit(solution)/shard_map/transpose(jvp())/reduce_sum | solution.py:12
  1590.0 41.1 %fusion.1 = (bf16[1,8192,768]{2,1,0:T(8,128)(2,1)}, bf16[1,8192,768]{2,1,0:T(8,128)(2,1)}) fusion(f32[1,8192,768]{2,1,0:T(8,128)} %copy.133, f32[32,768,256]{1,2,0:T(8,128)} %fusion.23, bf16[1,8192,768]{2,1,0:T(8,128)(2,1)} %param.17, bf16[1,8192,768]{2,1,0:T(8,128)(2,1)} %param.9, f32[8192]{0:T(1024)S(1)} %multiply_multiply_fusion, f32[8192]{0:T(1024)S(1)} %copy-done.3, ...), kind=kLoop, calls=%fused_computation.2 | loop fusion | flops 75497472 | bytes 125897728 | tf_op jit(solution)/shard_map/convert_element_type | solution.py:107
  (65 shorter events, 101.1 us)
Async XLA Ops:
  7.2 739.7 %copy-start = (bf16[768,384]{1,0:T(8,128)(2,1)S(1)}, bf16[768,384]{1,0:T(8,128)(2,1)}, u32[]{:S(2)}) copy-start(bf16[768,384]{1,0:T(8,128)(2,1)} %param.16) | copy-start | bytes 1769476
  14.4 14.4 copy-start.10
  28.7 443.7 %copy-start.1 = (f32[8192]{0:T(1024)}, f32[8192]{0:T(1024)S(1)}, u32[]{:S(2)}) copy-start(f32[8192]{0:T(1024)S(1)} %fusion.46) | copy-start | bytes 98308
  28.7 24.8 %copy-start.6 = (f32[32,256]{1,0:T(8,128)S(1)}, f32[32,256]{1,0:T(8,128)}, u32[]{:S(2)}) copy-start(f32[32,256]{1,0:T(8,128)} %param.12) | copy-start | bytes 98308
  28.7 24.8 %copy-start.8 = (bf16[256,256]{1,0:T(8,128)(2,1)S(1)}, bf16[256,256]{1,0:T(8,128)(2,1)}, u32[]{:S(2)}) copy-start(bf16[256,256]{1,0:T(8,128)(2,1)} %param.11) | copy-start | bytes 393220
  28.7 24.7 %copy-start.18 = (f32[768]{0:T(1024)S(1)}, f32[768]{0:T(1024)}, u32[]{:S(2)}) copy-start(f32[768]{0:T(1024)} %param.10) | copy-start | bytes 9220
  359.9 21.7 %copy-start.12 = (f32[128,64]{0,1:T(8,128)S(1)}, f32[128,64]{0,1:T(8,128)}, u32[]{:S(2)}) copy-start(f32[128,64]{0,1:T(8,128)} %param.14) | copy-start | bytes 98308
  359.9 21.7 %copy-start.16 = (bf16[128,128]{1,0:T(8,128)(2,1)S(1)}, bf16[128,128]{1,0:T(8,128)(2,1)}, u32[]{:S(2)}) copy-start(bf16[128,128]{1,0:T(8,128)(2,1)} %param.13) | copy-start | bytes 98308
  422.3 277.5 %all-to-all-start.1 = ((bf16[1,128,64,768]{3,2,0,1:T(8,128)(2,1)}), bf16[1,128,64,768]{3,2,0,1:T(8,128)(2,1)}, u32[]{:S(2)}, u32[]{:S(2)}) async-start(bf16[1,128,64,768]{3,2,0,1:T(8,128)(2,1)} %copy.112), calls=%async_computation.1 | async-start | bytes 25165824 | tf_op jit(solution)/shard_map/all_to_all | solution.py:43
  430.3 42.0 %copy-start.14 = (f32[2,384]{1,0:T(2,128)}, f32[2,384]{1,0:T(2,128)S(1)}, u32[]{:S(2)}) copy-start(f32[2,384]{1,0:T(2,128)S(1)} %mul.196) | copy-start | bytes 9220
  430.3 42.0 %copy-start.4 = (bf16[768,384]{1,0:T(8,128)(2,1)S(1)}, bf16[768,384]{1,0:T(8,128)(2,1)}, u32[]{:S(2)}) copy-start(bf16[768,384]{1,0:T(8,128)(2,1)} %param.15) | copy-start | bytes 1769476
  814.9 27.8 %copy-start.13 = (f32[128,64]{0,1:T(8,128)S(1)}, f32[128,64]{0,1:T(8,128)}, u32[]{:S(2)}) copy-start(f32[128,64]{0,1:T(8,128)} %param.14) | copy-start | bytes 98308
  833.1 279.0 %all-to-all-start.2 = ((bf16[1,32,256,768]{3,1,0,2:T(8,128)(2,1)}), bf16[1,32,256,768]{3,1,0,2:T(8,128)(2,1)}, u32[]{:S(2)}, u32[]{:S(2)}) async-start(bf16[1,32,256,768]{3,1,0,2:T(8,128)(2,1)} %copy.124), calls=%async_computation.2 | async-start | bytes 25165824 | tf_op jit(solution)/shard_map/all_to_all | solution.py:39
  1140.5 6.1 copy-start.17
  1186.1 350.9 %all-to-all-start.3 = ((bf16[1,128,64,768]{3,2,0,1:T(8,128)(2,1)}), bf16[1,128,64,768]{3,2,0,1:T(8,128)(2,1)}, u32[]{:S(2)}, u32[]{:S(2)}) async-start(bf16[1,128,64,768]{3,2,0,1:T(8,128)(2,1)} %copy.129), calls=%async_computation.3 | async-start | bytes 25165824 | tf_op jit(solution)/shard_map/all_to_all | solution.py:43
  1195.5 250.7 %reduce-scatter.2.cloned.1.call-start = ((), (), s32[]{:S(2)}) async-start(), calls=%async_computation.5 | async-start | bytes 2949120 | tf_op jit(solution)/shard_map/reduce_scatter | solution.py:108
  1195.5 14.0 copy-start.2
  1195.5 14.0 copy-start.15
  1209.5 17.4 %copy-start.5 = (bf16[768,384]{1,0:T(8,128)(2,1)S(1)}, bf16[768,384]{1,0:T(8,128)(2,1)}, u32[]{:S(2)}) copy-start(bf16[768,384]{1,0:T(8,128)(2,1)} %param.15) | copy-start | bytes 1769476
  1226.8 308.3 %all-reduce.2.cloned.1.call-start = ((), (), s32[]{:S(2)}) async-start(), calls=%async_computation.6 | async-start | bytes 1179648 | tf_op jit(solution)/shard_map/psum | solution.py:109
  1544.5 9.3 copy-start.7
  1544.5 9.3 copy-start.9
  1553.8 15.5 copy-start.19
  1569.3 20.7 %copy-start.11 = (f32[8192]{0:T(1024)S(1)}, f32[8192]{0:T(1024)}, u32[]{:S(2)}) copy-start(f32[8192]{0:T(1024)} %copy-done.10) | copy-start | bytes 98308
  1569.3 20.7 %copy-start.3 = (f32[8192]{0:T(1024)S(1)}, f32[8192]{0:T(1024)}, u32[]{:S(2)}) copy-start(f32[8192]{0:T(1024)} %copy-done.1) | copy-start | bytes 98308
Sparse Core Ops, SparseCore 0:
  1226.9 219.3 reduce-scatter.1
  1448.6 32.5 all-reduce.1
where the time goes:
time: 1650 us; the launch traced here: 1640 us
  waiting for transfers between devices  680 us (41%)
  local copies, waits for them, and re-layouts  327 us (20%)
  blocking collectives  276 us (17%)
  matrix products  197 us (12%)
  other arithmetic  117 us (7%)
  starting transfers between devices  27 us (2%)
    all_to_all x1, blocking collectives, to_columns(): lax.all_to_all(row_layout, 'seq', split_axis=2, concat_axis=1, tiled=True)  276 us
    all_to_all x1, waiting for transfers between devices, to_columns(): lax.all_to_all(row_layout, 'seq', split_axis=2, concat_axis=1, tiled=True)  269 us
    all_to_all x2, waiting for transfers between devices, to_rows(): lax.all_to_all(col_layout, 'seq', split_axis=1, concat_axis=2, tiled=True)  206 us
    reduce_scatter x1, waiting for transfers between devices, shards(): lax.psum_scatter(weight_term, 'seq', scatter_dimension=0, tiled=True)  205 us
    dot_general x2, matrix products, block_back(): jnp.einsum('rkj,kij->rki', grouped, stacked, preferred_element_type=jnp.f...  54.5 us
    reshape x2, local copies, waits for them, and re-layouts, block_back(): return result.reshape(partner.shape[0], -1)  49.5 us
    convert_element_type x2, local copies, waits for them, and re-layouts, shards(): inputs_wide = inputs.reshape(flat_rows, channels).astype(jnp.float32)  42.4 us
    convert_element_type x1, other arithmetic, shards(): (cotan_rows.astype(jnp.float32) + pullback(act_grad)[0]).astype(jnp.bfloa...  41.1 us
  transfers between devices with their start and end apart: 5, of which 3 were waited for; matrix products, arithmetic and copies ran while one was open for 12% of the time, Pallas kernels for 0%

commit v1 on v0

--- a/solution.py
+++ b/solution.py
@@ -36,7 +36,10 @@
 
 
 def to_columns(row_layout):
-    return lax.all_to_all(row_layout, "seq", split_axis=2, concat_axis=1, tiled=True)
+    return jnp.concatenate(
+        lax.all_to_all(jnp.stack(jnp.split(row_layout, lax.axis_size("seq"), axis=2)), "seq", 0, 0),
+        axis=1,
+    )
 
 
 def to_rows(col_layout):

time: 1650 us -> 1610 us (0.976)
  local copies, waits for them, and re-layouts: 327 us -> 267 us
  other arithmetic: 117 us -> 137 us
    another operation x0 -> x3, local copies, waits for them, and re-layouts: none -> 43.7 us  [to_columns(): jnp.stack(jnp.split(row_layout, lax.axis_size('seq'), axis=2))]
    all_to_all x3 -> x0, local copies, waits for them, and re-layouts: 30.7 us -> none  [to_columns(): lax.all_to_all(row_layout, 'seq', split_axis=2, concat_axis=1, tiled=True)]
    convert_element_type x2 -> x0, local copies, waits for them, and re-layouts: 26.6 us -> none  [the longest x1 16.6 us: shards(): mixed_rows = (inner_out * twiddle[None, :, :, None]).astype(jnp.bfloat16)]
    convert_element_type x2 -> x1, local copies, waits for them, and re-layouts: 42.4 us -> 17.6 us  [shards(): inputs_wide = inputs.reshape(flat_rows, channels).astype(jnp.float32)]
    another operation x0 -> x2, other arithmetic: none -> 23.9 us  [to_columns(): jnp.stack(jnp.split(row_layout, lax.axis_size('seq'), axis=2))]
    convert_element_type x2 -> x1, local copies, waits for them, and re-layouts: 34.4 us -> 16.8 us  [shards(): mix_grad = (back_gated * gate_pre * gate_sig).astype(jnp.bfloat16)]
  transfers between devices with their start and end apart: 5 -> 5, of which waited for: 3 -> 3; matrix products, arithmetic and copies ran while one was open for 12% -> 13% of each run, Pallas kernels for 0% -> 0%
where the time goes in v1:
time: 1610 us; the launch traced here: 1600 us
  waiting for transfers between devices  680 us (42%)
  blocking collectives  276 us (17%)
  local copies, waits for them, and re-layouts  267 us (17%)
  matrix products  197 us (12%)
  other arithmetic  137 us (9%)
  starting transfers between devices  27 us (2%)
    all_to_all x1, blocking collectives, to_columns(): lax.all_to_all(jnp.stack(jnp.split(row_layout, lax.axis_size('seq'), axis...  276 us
    all_to_all x1, waiting for transfers between devices, to_columns(): lax.all_to_all(jnp.stack(jnp.split(row_layout, lax.axis_size('seq'), axis...  269 us
    all_to_all x2, waiting for transfers between devices, to_rows(): lax.all_to_all(col_layout, 'seq', split_axis=1, concat_axis=2, tiled=True)  206 us
    reduce_scatter x1, waiting for transfers between devices, shards(): lax.psum_scatter(weight_term, 'seq', scatter_dimension=0, tiled=True)  204 us
    dot_general x2, matrix products, block_back(): jnp.einsum('rkj,kij->rki', grouped, stacked, preferred_element_type=jnp.f...  54.7 us
    reshape x2, local copies, waits for them, and re-layouts, block_back(): return result.reshape(partner.shape[0], -1)  49.5 us
    another operation x3, local copies, waits for them, and re-layouts, to_columns(): jnp.stack(jnp.split(row_layout, lax.axis_size('seq'), axis=2))  43.7 us
    convert_element_type x1, other arithmetic, shards(): (cotan_rows.astype(jnp.float32) + pullback(act_grad)[0]).astype(jnp.bfloa...  41.1 us
  transfers between devices with their start and end apart: 5, of which 3 were waited for; matrix products, arithmetic and copies ran while one was open for 13% of the time, Pallas kernels for 0%

profile of v1, /device:TPU:21, one launch (start us, length us, event | category | flops | bytes accessed | tf_op | source)
XLA Modules:
  0.0 1598.0 jit_solution(15134747082382316010)
XLA Ops:
  14.4 14.3 convert_element_type.129
  28.8 13.8 fusion.24
  49.8 275.6 %all_to_all.28 = bf16[4,1,32,64,768]{4,3,2,1,0:T(8,128)(2,1)} all-to-all(bf16[4,1,32,64,768]{4,3,2,1,0:T(8,128)(2,1)S(1)} %pad_maximum_fusion.1), channel_id=1, replica_groups=mesh['groups'=2,'seq'=4,'dp'=4] {'seq'}, dimensions={0} | all-to-all | bytes 25165824 | tf_op jit(solution)/shard_map/all_to_all | solution.py:40
  325.4 24.2 %fusion.8 = bf16[1,128,64,768]{1,3,2,0:T(8,128)(2,1)} fusion(f32[128,64]{0,1:T(8,128)S(1)} %copy-done.12, bf16[128,64,768]{2,1,0:T(8,128)(2,1)} %bitcast.168, bf16[128,128]{1,0:T(8,128)(2,1)S(1)} %copy-done.16), kind=kOutput, calls=%fused_computation.16 | convolution fusion | flops 1623195648 | bytes 25231360 | tf_op jit(solution)/shard_map/ip,bpjd->bijd/dot_general | solution.py:76
  349.6 16.5 %copy.76 = bf16[1,128,64,768]{3,2,0,1:T(8,128)(2,1)} copy(bf16[1,128,64,768]{1,3,2,0:T(8,128)(2,1)} %fusion.8) | data formatting | bytes 25165824 | tf_op jit(solution)/shard_map/convert_element_type | solution.py:77
  374.2 17.6 %copy.107 = f32[1,8192,768]{1,2,0:T(8,128)} copy(bf16[1,8192,768]{2,1,0:T(8,128)(2,1)} %param.9) | data formatting | bytes 37748736 | tf_op jit(solution)/shard_map/convert_element_type | solution.py:68
  391.8 24.4 %reshape_reshape.4 = bf16[8192,2,384]{2,1,0:T(2,128)(2,1)} reshape(bf16[1,8192,768]{2,1,0:T(8,128)(2,1)} %param.17) | data formatting | bytes 25165824 | tf_op jit(solution)/shard_map/reshape;reshape | solution.py:25
  416.2 21.1 %fusion.41 = f32[2,8192,384]{2,1,0:T(8,128)} fusion(bf16[2,384,384]{2,1,0:T(8,128)(2,1)S(1)} %bitcast.171, f32[8192,2,384]{0,2,1:T(8,128)} %bitcast.162, f32[2,384]{1,0:T(2,128)S(1)} %mul.196, f32[8192]{0:T(1024)S(1)} %fusion.46), kind=kOutput, calls=%fused_computation.62 | convolution fusion | flops 4850712576 | bytes 50957312 | tf_op jit(solution)/shard_map/rki,kij->rkj/dot_general | solution.py:19
  437.3 206.3 %all-to-all-done.1 = bf16[1,128,64,768]{3,2,0,1:T(8,128)(2,1)} async-done(((bf16[1,128,64,768]{3,2,0,1:T(8,128)(2,1)}), bf16[1,128,64,768]{3,2,0,1:T(8,128)(2,1)}, u32[]{:S(2)}, u32[]{:S(2)}) %all-to-all-start.1) | async-done | bytes 12582944 | tf_op jit(solution)/shard_map/all_to_all | solution.py:46
  660.3 30.3 %reshape.272 = f32[8192,2,384]{2,1,0:T(2,128)} reshape(f32[1,32,4,64,768]{4,3,2,1,0:T(8,128)} %copy.78) | data formatting | bytes 50331648 | tf_op jit(solution)/shard_map/convert_element_type | solution.py:81
  690.6 39.8 %fusion.13 = (bf16[8192,2,384]{2,0,1:T(8,128)(2,1)}, bf16[8192,2,384]{2,0,1:T(8,128)(2,1)}, bf16[8192,2,384]{2,0,1:T(8,128)(2,1)}) fusion(f32[2,8192,384]{2,1,0:T(8,128)} %fusion.41, f32[8192,2,384]{2,1,0:T(2,128)} %reshape.272, bf16[2,384,384]{2,1,0:T(8,128)(2,1)S(1)} %bitcast.159, bf16[8192,2,384]{2,1,0:T(2,128)(2,1)} %reshape_reshape.4), kind=kOutput, calls=%fused_computation.23 | convolution fusion | flops 4932501504 | bytes 101253120 | tf_op jit(solution)/shard_map/rkj,kij->rki/dot_general | solution.py:27
  730.4 16.8 %copy.87 = bf16[8192,2,384]{0,2,1:T(8,128)(2,1)} copy(bf16[8192,2,384]{2,0,1:T(8,128)(2,1)} %get-tuple-element.3) | data formatting | bytes 25165824 | tf_op jit(solution)/shard_map/convert_element_type | solution.py:86
  755.3 9.9 slice_bitcast_fusion.3
  765.2 22.2 %pad_maximum_fusion = bf16[4,1,32,64,768]{3,2,4,1,0:T(8,128)(2,1)} fusion(bf16[1,1,32,64,768]{3,2,4,1,0:T(8,128)(2,1)} %get-tuple-element.9, bf16[1,1,32,64,768]{3,2,4,1,0:T(8,128)(2,1)} %get-tuple-element.10, bf16[1,1,32,64,768]{3,2,4,1,0:T(8,128)(2,1)} %get-tuple-element.11, bf16[1,1,32,64,768]{3,2,4,1,0:T(8,128)(2,1)} %get-tuple-element.8), kind=kLoop, calls=%fused_computation.3 | loop fusion | flops 18874368 | bytes 25165824 | tf_op jit(solution)/shard_map/stack | solution.py:40
  787.4 28.4 %copy.90 = bf16[4,1,32,64,768]{4,3,2,1,0:T(8,128)(2,1)} copy(bf16[4,1,32,64,768]{3,2,4,1,0:T(8,128)(2,1)} %pad_maximum_fusion) | data formatting | bytes 25165824 | tf_op jit(solution)/shard_map/stack | solution.py:40
  815.8 9.5 all-to-all-start.2
  825.5 269.4 %all-to-all-done.2 = bf16[4,1,32,64,768]{4,3,2,1,0:T(8,128)(2,1)} async-done(((bf16[4,1,32,64,768]{4,3,2,1,0:T(8,128)(2,1)}), bf16[4,1,32,64,768]{4,3,2,1,0:T(8,128)(2,1)}, u32[]{:S(2)}, u32[]{:S(2)}) %all-to-all-start.2) | async-done | bytes 12582944 | tf_op jit(solution)/shard_map/all_to_all | solution.py:40
  1094.8 11.6 fusion.7
  1106.4 22.8 %convert_bitcast_fusion.2 = bf16[1,128,64,768]{1,3,2,0:T(8,128)(2,1)} fusion(bf16[128,64,768]{2,1,0:T(8,128)(2,1)} %fusion.7, bf16[128,128]{1,0:T(8,128)(2,1)S(1)} %copy-done.17), kind=kOutput, calls=%fused_computation.50 | convolution fusion | flops 1616904192 | bytes 25198592 | tf_op jit(solution)/shard_map/ip,bijd->bpjd/dot_general | solution.py:102
  1129.2 16.5 %copy.94 = bf16[1,128,64,768]{3,2,0,1:T(8,128)(2,1)} copy(bf16[1,128,64,768]{1,3,2,0:T(8,128)(2,1)} %convert_bitcast_fusion.2) | data formatting | bytes 25165824 | tf_op jit(solution)/shard_map/convert_element_type | solution.py:104
  1145.7 9.4 all-to-all-start.3
  1155.1 14.1 fusion.32
  1169.3 15.7 fusion.40
  1186.6 14.9 fusion.48
  1201.5 204.3 %reduce-scatter.2.cloned.1.call-done = f32[384,384]{1,0:T(8,128)} async-done(((f32[1536,384]{1,0:T(8,128)}), f32[384,384]{1,0:T(8,128)}) %reduce-scatter.2.cloned.1.call-update) | async-done | bytes 589840 | tf_op jit(solution)/shard_map/reduce_scatter | solution.py:111
  1405.9 14.7 fusion.47
  1420.5 24.8 %copy.99 = f32[8192,768]{1,0:T(8,128)} copy(f32[8192,768]{0,1:T(8,128)} %bitcast.160) | data formatting | bytes 50331648 | tf_op jit(solution)/shard_map/reshape | solution.py:28
  1445.3 24.7 %copy.98 = f32[1,8192,768]{2,1,0:T(8,128)} copy(f32[1,8192,768]{1,2,0:T(8,128)} %bitcast.161) | data formatting | bytes 50331648 | tf_op jit(solution)/shard_map/reshape | solution.py:28
  1470.0 24.7 %copy.83 = f32[1,8192,768]{2,1,0:T(8,128)} copy(f32[1,8192,768]{1,2,0:T(8,128)} %bitcast.165) | data formatting | bytes 50331648 | tf_op jit(solution)/shard_map/reshape | solution.py:20
  1513.3 15.5 fusion.23
  1528.9 20.7 %fusion.4 = f32[8192]{0:T(1024)S(1)} fusion(f32[8192,768]{1,0:T(8,128)} %copy.99, f32[32,768,256]{1,2,0:T(8,128)} %fusion.23, bf16[1,8192,768]{2,1,0:T(8,128)(2,1)} %param.9, f32[768]{0:T(1024)S(1)} %copy-done.19), kind=kLoop, calls=%fused_computation.7 | loop fusion | flops 31449088 | bytes 62950400 | tf_op jit(solution)/shard_map/transpose(jvp())/reduce_sum | solution.py:12
  1549.6 41.1 %fusion.1 = (bf16[1,8192,768]{2,1,0:T(8,128)(2,1)}, bf16[1,8192,768]{2,1,0:T(8,128)(2,1)}) fusion(f32[1,8192,768]{2,1,0:T(8,128)} %copy.98, f32[32,768,256]{1,2,0:T(8,128)} %fusion.23, bf16[1,8192,768]{2,1,0:T(8,128)(2,1)} %param.17, bf16[1,8192,768]{2,1,0:T(8,128)(2,1)} %param.9, f32[8192]{0:T(1024)S(1)} %multiply_multiply_fusion, f32[8192]{0:T(1024)S(1)} %copy-done.3, ...), kind=kLoop, calls=%fused_computation.2 | loop fusion | flops 75497472 | bytes 125897728 | tf_op jit(solution)/shard_map/convert_element_type | solution.py:110
  (62 shorter events, 67.6 us)
Async XLA Ops:
  7.2 683.5 %copy-start = (bf16[768,384]{1,0:T(8,128)(2,1)S(1)}, bf16[768,384]{1,0:T(8,128)(2,1)}, u32[]{:S(2)}) copy-start(bf16[768,384]{1,0:T(8,128)(2,1)} %param.16) | copy-start | bytes 1769476
  14.4 14.4 copy-start.10
  14.4 14.4 copy-start.6
  14.4 14.4 copy-start.8
  14.4 14.4 copy-start.18
  28.7 387.4 %copy-start.1 = (f32[8192]{0:T(1024)}, f32[8192]{0:T(1024)S(1)}, u32[]{:S(2)}) copy-start(f32[8192]{0:T(1024)S(1)} %fusion.46) | copy-start | bytes 98308
  49.7 275.6 %copy-start.12 = (f32[128,64]{0,1:T(8,128)S(1)}, f32[128,64]{0,1:T(8,128)}, u32[]{:S(2)}) copy-start(f32[128,64]{0,1:T(8,128)} %param.14) | copy-start | bytes 98308
  49.8 275.6 %copy-start.16 = (bf16[128,128]{1,0:T(8,128)(2,1)S(1)}, bf16[128,128]{1,0:T(8,128)(2,1)}, u32[]{:S(2)}) copy-start(bf16[128,128]{1,0:T(8,128)(2,1)} %param.13) | copy-start | bytes 98308
  366.1 277.5 %all-to-all-start.1 = ((bf16[1,128,64,768]{3,2,0,1:T(8,128)(2,1)}), bf16[1,128,64,768]{3,2,0,1:T(8,128)(2,1)}, u32[]{:S(2)}, u32[]{:S(2)}) async-start(bf16[1,128,64,768]{3,2,0,1:T(8,128)(2,1)} %copy.76), calls=%async_computation.1 | async-start | bytes 25165824 | tf_op jit(solution)/shard_map/all_to_all | solution.py:46
  374.1 42.0 %copy-start.14 = (f32[2,384]{1,0:T(2,128)}, f32[2,384]{1,0:T(2,128)S(1)}, u32[]{:S(2)}) copy-start(f32[2,384]{1,0:T(2,128)S(1)} %mul.196) | copy-start | bytes 9220
  391.8 24.4 %copy-start.4 = (bf16[768,384]{1,0:T(8,128)(2,1)S(1)}, bf16[768,384]{1,0:T(8,128)(2,1)}, u32[]{:S(2)}) copy-start(bf16[768,384]{1,0:T(8,128)(2,1)} %param.15) | copy-start | bytes 1769476
  815.8 9.5 copy-start.13
  815.8 279.0 %all-to-all-start.2 = ((bf16[4,1,32,64,768]{4,3,2,1,0:T(8,128)(2,1)}), bf16[4,1,32,64,768]{4,3,2,1,0:T(8,128)(2,1)}, u32[]{:S(2)}, u32[]{:S(2)}) async-start(bf16[4,1,32,64,768]{4,3,2,1,0:T(8,128)(2,1)} %copy.90), calls=%async_computation.2 | async-start | bytes 25165824 | tf_op jit(solution)/shard_map/all_to_all | solution.py:40
  825.5 281.0 %copy-start.17 = (bf16[128,128]{1,0:T(8,128)(2,1)S(1)}, bf16[128,128]{1,0:T(8,128)(2,1)}, u32[]{:S(2)}) copy-start(bf16[128,128]{1,0:T(8,128)(2,1)} %param.13) | copy-start | bytes 98308
  1145.7 350.9 %all-to-all-start.3 = ((bf16[1,128,64,768]{3,2,0,1:T(8,128)(2,1)}), bf16[1,128,64,768]{3,2,0,1:T(8,128)(2,1)}, u32[]{:S(2)}, u32[]{:S(2)}) async-start(bf16[1,128,64,768]{3,2,0,1:T(8,128)(2,1)} %copy.94), calls=%async_computation.3 | async-start | bytes 25165824 | tf_op jit(solution)/shard_map/all_to_all | solution.py:46
  1155.1 250.7 %reduce-scatter.2.cloned.1.call-start = ((), (), s32[]{:S(2)}) async-start(), calls=%async_computation.5 | async-start | bytes 2949120 | tf_op jit(solution)/shard_map/reduce_scatter | solution.py:111
  1155.1 14.1 copy-start.2
  1155.1 14.1 copy-start.15
  1169.3 17.3 %copy-start.5 = (bf16[768,384]{1,0:T(8,128)(2,1)S(1)}, bf16[768,384]{1,0:T(8,128)(2,1)}, u32[]{:S(2)}) copy-start(bf16[768,384]{1,0:T(8,128)(2,1)} %param.15) | copy-start | bytes 1769476
  1186.6 308.1 %all-reduce.2.cloned.1.call-start = ((), (), s32[]{:S(2)}) async-start(), calls=%async_computation.6 | async-start | bytes 1179648 | tf_op jit(solution)/shard_map/psum | solution.py:112
  1504.0 9.3 copy-start.7
  1504.1 9.3 copy-start.9
  1513.3 15.5 copy-start.19
  1528.8 20.7 %copy-start.11 = (f32[8192]{0:T(1024)S(1)}, f32[8192]{0:T(1024)}, u32[]{:S(2)}) copy-start(f32[8192]{0:T(1024)} %copy-done.10) | copy-start | bytes 98308
  1528.8 20.7 %copy-start.3 = (f32[8192]{0:T(1024)S(1)}, f32[8192]{0:T(1024)}, u32[]{:S(2)}) copy-start(f32[8192]{0:T(1024)} %copy-done.1) | copy-start | bytes 98308
Sparse Core Ops, SparseCore 0:
  1186.7 219.0 reduce-scatter.1
  1408.2 32.6 all-reduce.1
